TPU v7x, 256 devices: a whole 4x4x8 slice. The times are simulated.
256 devices in a mesh: dp: 32 (over z, x_hi, core), space: 8 (over x_lo, y).
Axes of the slice: x: 4 (x_hi: 2, x_lo: 2; x = x_hi * 2 + x_lo), y: 4, z: 8, core: 2. Of those that a mesh axis runs over, the one named last changes fastest.
Arguments:
- volume: bfloat16 [256, 4, 32, 16, 128], P('dp', None, 'space'), may hold values from -8 to 8
- conv_kernel: bfloat16 [32, 108], replicated, may hold values from -0.625 to 0.625
- dense_weight: bfloat16 [512, 128], replicated, may hold values from -0.25 to 0.25
- cotangent: bfloat16 [256, 128], P(('dp', 'space')), may hold values from -6 to 6
Outputs:
- step_conv: float32 [32, 108], replicated
- step_dense: float32 [512, 128], P('space', 'dp')
All inputs are finite; a program needn't handle non-finite values. Where the computation divides by a largest or mean magnitude, that divisor is 1e-20 or more.
Results may differ from a plain program's by a relative error of at most 0.0099.
Values may be sent and summed in bfloat16 or wider, within the bound.
No kernel may reach another device: no remote copies, remote signals or barrier semaphores. Data moves between devices by JAX's collectives and lax.ppermute only.
A program may use at most 64 MiB of HBM per device.

v0:
```python
import jax
import jax.numpy as jnp
from jax import lax
from jax.sharding import PartitionSpec as P

PC = 2
NS_STEPS = 8
LEAK_SLOPE = 0.3
DAMPING = 0.1
KL_BOUND = 0.0001
LEARN_RATE = 0.01
HIGHEST = lax.Precision.HIGHEST
CONTRACT = (((1,), (1,)), ((), ()))
LEADING = (((0,), (0,)), ((), ()))


def spread_2(value, axis, source):
    kept = jnp.where(lax.axis_index(axis) == source, value, 0).astype(value.dtype)
    return lax.psum(kept, axis)


def extended(x, sides, width):
    for axis, dim in sides:
        peers, length = (lax.axis_size(axis), x.shape[dim])
        up = [(i, (i + 1) % peers) for i in range(peers - 1)]
        down = [(j, i) for i, j in up]
        last = lax.slice_in_dim(x, length - width, length, axis=dim)
        initial = lax.slice_in_dim(x, 0, width, axis=dim)
        before = lax.ppermute(last, axis, up)
        after = lax.ppermute(initial, axis, down)
        x = jnp.concatenate([before, x, after], axis=dim)
    return x


def patch_matrix(slab_rim):
    channels, planes_rim, height, length = slab_rim.shape
    planes = planes_rim - 2
    padded = jnp.pad(slab_rim, ((0, 0), (0, 0), (1, 1), (1, 1)))
    pieces = []
    for shift_x in range(3):
        for shift_y in range(3):
            for shift_z in range(3):
                pieces.append(
                    padded[
                        :,
                        shift_x : shift_x + planes,
                        shift_y : shift_y + height,
                        shift_z : shift_z + length,
                    ]
                )
    return jnp.stack(pieces, axis=1).reshape(channels * 27, planes * height * length)


def damped_inverse(factor):
    factor_order = factor.shape[0]
    identity = jnp.eye(factor_order, dtype=jnp.float32)
    damped = factor + DAMPING * jnp.trace(factor) / factor_order * identity
    row_bound = jnp.max(jnp.sum(jnp.abs(damped), axis=1))
    iterate = identity / row_bound
    for newton_step in range(NS_STEPS):
        product = jnp.dot(damped, iterate, precision=HIGHEST)
        iterate = jnp.dot(iterate, 2.0 * identity - product, precision=HIGHEST)
    return iterate


def owned_inverse(factor, owner_index):
    mine = lax.axis_index("dp") == owner_index
    local_inverse = lax.cond(mine, damped_inverse, jnp.zeros_like, factor)
    return spread_2(local_inverse, "dp", owner_index)


def pool_regions(active, planes, height, length):
    shaped = active.reshape(active.shape[0], planes, PC, height // PC, length)
    return jnp.mean(shaped, axis=(1, 3, 4)).reshape(-1)


def dense_moments_of(features, cotangent):
    dense_in = lax.dot_general(features, features, LEADING, preferred_element_type=jnp.float32)
    dense_out = lax.dot_general(cotangent, cotangent, LEADING, preferred_element_type=jnp.float32)
    dense_grad = lax.dot_general(features, cotangent, LEADING, preferred_element_type=jnp.float32)
    return (dense_in, dense_out, dense_grad)


def on_device(volume, conv_kernel, dense_weight, cotangent):
    spaces = lax.axis_size("space")
    groups = lax.axis_size("dp")
    samples, channels, planes, height, length = volume.shape
    filters = conv_kernel.shape[0]
    patch_rows = conv_kernel.shape[1]
    padded = extended(volume, (("space", 2),), 1)

    def forward_pass(moment_in, slab_rim):
        patches = patch_matrix(slab_rim)
        before = jnp.dot(conv_kernel, patches, preferred_element_type=jnp.float32)
        active = jnp.where(before > 0, before, LEAK_SLOPE * before)
        pooled = pool_regions(active, planes, height, length).astype(jnp.bfloat16)
        gram = lax.dot_general(patches, patches, CONTRACT, preferred_element_type=jnp.float32)
        return (moment_in + gram, pooled)

    moment_in, pooled_all = lax.scan(
        forward_pass, jnp.zeros((patch_rows, patch_rows), jnp.float32), padded
    )
    features = lax.all_to_all(pooled_all, "space", split_axis=0, concat_axis=1, tiled=True)
    feature_grad = lax.dot_general(
        cotangent, dense_weight, CONTRACT, preferred_element_type=jnp.float32
    ).astype(jnp.bfloat16)
    returned = lax.all_to_all(feature_grad, "space", split_axis=1, concat_axis=0, tiled=True)

    def backward_pass(totals, pair):
        slab_rim, region_grad = pair
        patches = patch_matrix(slab_rim)
        before = jnp.dot(conv_kernel, patches, preferred_element_type=jnp.float32)
        region_grid = region_grad.astype(jnp.float32).reshape(filters, 1, PC, 1, 1)
        spread = jnp.broadcast_to(region_grid, (filters, planes, PC, height // PC, length)).reshape(
            filters, -1
        )
        signal = (jnp.where(before > 0, 1.0, LEAK_SLOPE) * spread).astype(jnp.bfloat16)
        moment_out = totals[0] + lax.dot_general(
            signal, signal, CONTRACT, preferred_element_type=jnp.float32
        )
        gradient = totals[1] + lax.dot_general(
            signal, patches, CONTRACT, preferred_element_type=jnp.float32
        )
        return ((moment_out, gradient), None)

    start_totals = (
        jnp.zeros((filters, filters), jnp.float32),
        jnp.zeros((filters, patch_rows), jnp.float32),
    )
    (moment_out, conv_sum), unused = lax.scan(backward_pass, start_totals, (padded, returned))
    conv_in, conv_out, conv_grad = lax.psum((moment_in, moment_out, conv_sum), ("dp", "space"))
    total_samples = samples * groups
    cell_count = total_samples * planes * spaces * height * length
    conv_in = conv_in / cell_count
    conv_out = conv_out / cell_count
    conv_grad = conv_grad / cell_count
    all_features, all_cotangent = (
        lax.all_gather(features, ("dp", "space"), axis=0, tiled=True),
        lax.all_gather(cotangent, ("dp", "space"), axis=0, tiled=True),
    )
    dense_in, dense_out, dense_grad = dense_moments_of(all_features, all_cotangent)
    dense_in = dense_in / total_samples
    dense_out = dense_out / total_samples
    dense_grad = dense_grad / total_samples
    factors = (conv_in, conv_out, dense_in, dense_out)
    stride = groups // len(factors)
    inverses = []
    for place in range(4):
        inverses.append(owned_inverse(factors[place], place * stride))
    inv_conv_in, inv_conv_out, inv_dense_in, inv_dense_out = inverses
    delta_conv = jnp.dot(
        jnp.dot(inv_conv_out, conv_grad, precision=HIGHEST), inv_conv_in, precision=HIGHEST
    )
    conv_total = jnp.sum(delta_conv * conv_grad)
    delta_whole = jnp.dot(
        jnp.dot(inv_dense_in, dense_grad, precision=HIGHEST), inv_dense_out, precision=HIGHEST
    )
    dense_total = jnp.sum(delta_whole * dense_grad)
    share_rows = dense_grad.shape[0] // spaces
    share_cols = dense_grad.shape[1] // groups
    first_row = lax.axis_index("space") * share_rows
    first_col = lax.axis_index("dp") * share_cols
    delta_rows = lax.dynamic_slice_in_dim(delta_whole, first_row, share_rows, 0)
    delta_block = lax.dynamic_slice_in_dim(delta_rows, first_col, share_cols, 1)
    scaling = jnp.minimum(
        1.0, jnp.sqrt(KL_BOUND / (LEARN_RATE * LEARN_RATE * (conv_total + dense_total)))
    )
    return (scaling * delta_conv, scaling * delta_block)


def solution(mesh):
    placed = (P("dp", None, "space", None, None), P(), P(), P(("dp", "space"), None))
    return jax.shard_map(
        on_device, mesh=mesh, in_specs=placed, out_specs=(P(), P("space", "dp")), check_vma=False
    )
```

profile of v0, /device:TPU:2, one launch (start us, length us, event | category | flops | bytes accessed | tf_op | source)
XLA Modules:
  0.0 2039.7 jit_solution(5955070597931003601)
XLA Ops:
  7.2 1.0 fusion.162
  8.2 3.5 collective-permute-start
  11.7 4.5 collective-permute-start.1
  17.7 3.8 all-to-all-start
  21.5 619.8 %all-gather.1 = bf16[256,1,128]{2,1,0:T(2,128)(2,1)S(1)} all-gather(bf16[1,1,128]{2,1,0:T(2,128)(2,1)} %bitcast.621), channel_id=1, replica_groups=mesh['dp'=32,'space'=8] {'dp','space'}, dimensions={0}, use_global_device_ids=true | all-gather | bytes 65792 | tf_op jit(solution)/shard_map/all_gather | solution.py:139
  642.7 190.2 %while.30 = (s32[]{:T(128)}, f32[32,32]{1,0:T(8,128)S(1)}, f32[32,108]{1,0:T(8,128)S(1)}, bf16[8,4,6,16,128]{4,3,2,1,0:T(8,128)(2,1)S(1)}, bf16[32,108]{1,0:T(8,...) while((s32[]{:T(128)}, f32[32,32]{1,0:T(8,128)S(1)}, ...), condition=%wide.region_1.2_spmd.clone, body=%wide.region_0.1_spmd.clone.sunk | while | flops 131081024 | bytes 15313904 | solution.py:130
  661.6 2.7 reshape.103
  685.3 2.7 reshape.103
  709.1 2.7 reshape.103
  732.9 2.7 reshape.103
  756.7 2.7 reshape.103
  780.5 2.7 reshape.103
  804.2 2.7 reshape.103
  828.0 2.7 reshape.103
  832.9 185.2 %while.31 = (s32[]{:T(128)}, f32[108,108]{1,0:T(8,128)S(1)}, bf16[8,64]{1,0:T(8,128)(2,1)S(1)}, bf16[8,4,6,16,128]{4,3,2,1,0:T(8,128)(2,1)S(1)}, bf16[32,108]{1,...) while((s32[]{:T(128)}, f32[108,108]{1,0:T(8,128)S(1)}, bf16[8,64]{1,0:T(8,128)(2,1)S(1)}, ...), condition=%wide.region_12.13_spmd.clone, body=%wide.region_10.12_spmd.clone.sunk | while | flops 248798048 | bytes 15895667 | solution.py:100
  851.8 2.7 reshape.105
  874.9 2.7 reshape.105
  898.1 2.7 reshape.105
  921.2 2.7 reshape.105
  944.4 2.7 reshape.105
  967.6 2.7 reshape.105
  990.7 2.7 reshape.105
  1013.9 2.7 reshape.105
  1018.7 12.3 all-to-all-start.1
  1031.0 73.1 %all-reduce.2 = (f32[32,32]{1,0:T(8,128)S(1)}, f32[32,108]{1,0:T(8,128)S(1)}, f32[108,108]{1,0:T(8,128)S(1)}) all-reduce(f32[32,32]{1,0:T(8,128)S(1)} %get-tuple-element.174, f32[32,108]{1,0:T(8,128)S(1)} %get-tuple-element.175, f32[108,108]{1,0:T(8,128)S(1)} %get-tuple-element.176), channel_id=1, replica_groups=mesh['dp'=32,'space'=8] {'dp','space'}, use_global_device_ids=true, to_apply=%region_2.3 | all-reduce | flops 16144 | bytes 129152 | tf_op jit(solution)/shard_map/psum | solution.py:131
  1104.2 6.2 conditional.5
  1110.4 614.5 %all-gather = bf16[256,1,512]{2,1,0:T(2,128)(2,1)S(1)} all-gather(bf16[1,1,512]{2,1,0:T(2,128)(2,1)S(1)} %reshape.80), channel_id=1, replica_groups=mesh['dp'=32,'space'=8] {'dp','space'}, dimensions={0}, use_global_device_ids=true | all-gather | bytes 263168 | tf_op jit(solution)/shard_map/all_gather | solution.py:138
  1725.7 1.1 broadcast_select_fusion
  1726.8 129.0 %all-reduce.3 = (f32[32,32]{1,0:T(8,128)S(1)}, f32[108,108]{1,0:T(8,128)S(1)}) all-reduce(f32[32,32]{1,0:T(8,128)S(1)} %broadcast_select_fusion.3, f32[108,108]{1,0:T(8,128)S(1)} %broadcast_select_fusion.2), channel_id=1, replica_groups=mesh['dp'=32,'space'=8] {'dp'}, use_global_device_ids=true, to_apply=%region_8.9 | all-reduce | flops 12688 | bytes 101504 | tf_op jit(solution)/shard_map/psum | solution.py:19
  1857.0 168.8 %all-reduce.7.cloned.1.call-done = (f32[512,512]{1,0:T(8,128)}, f32[128,128]{1,0:T(8,128)}) async-done(((f32[512,512]{1,0:T(8,128)}, f32[128,128]{1,0:T(8,128)}), (f32[512,512]{1,0:T(8,128)}, f32[128,128]{1,0:T(8,128)})) %all-reduce.7.cloned.1.call-update) | async-done | bytes 1114128 | tf_op jit(solution)/shard_map/psum | solution.py:19
  2025.9 2.2 fusion.191
  2028.1 1.3 fusion.192
  (615 shorter events, 343.1 us)
Async XLA Ops:
  7.2 9.0 copy-start
  8.2 634.0 %collective-permute-start = (bf16[8,4,1,16,128]{4,3,2,1,0:T(8,128)(2,1)S(1)}, bf16[8,4,1,16,128]{4,3,2,1,0:T(8,128)(2,1)S(1)}, u32[]{:S(2)}, u32[]{:S(2)}) collective-permute-start(bf16[8,4,1,16,128]{4,3,2,1,0:T(8,128)(2,1)S(1)} %get-tuple-element.247), channel_id=1, source_target_pairs={{0,1},{1,2},{2,3},{3,4},{4,5},{5,6},{6,7},{8,9},{9,10},{10,11},{11... | collective-permute-start | bytes 393224 | tf_op jit(solution)/shard_map/ppermute | solution.py:29
  11.7 631.0 %collective-permute-start.1 = (bf16[8,4,1,16,128]{4,3,2,1,0:T(8,128)(2,1)S(1)}, bf16[8,4,1,16,128]{4,3,2,1,0:T(8,128)(2,1)S(1)}, u32[]{:S(2)}, u32[]{:S(2)}) collective-permute-start(bf16[8,4,1,16,128]{4,3,2,1,0:T(8,128)(2,1)S(1)} %get-tuple-element.246), channel_id=1, source_target_pairs={{1,0},{2,1},{3,2},{4,3},{5,4},{6,5},{7,6},{9,8},{10,9},{11,10},{12... | collective-permute-start | bytes 393224 | tf_op jit(solution)/shard_map/ppermute | solution.py:30
  17.7 624.5 %all-to-all-start = ((bf16[1,8,64]{2,0,1:T(2,128)(2,1)}), bf16[1,8,64]{2,0,1:T(2,128)(2,1)S(1)}, u32[]{:S(2)}, u32[]{:S(2)}) async-start(bf16[1,8,64]{2,0,1:T(2,128)(2,1)} %all_to_all.30), calls=%async_computation | async-start | bytes 8192 | tf_op jit(solution)/shard_map/all_to_all | solution.py:107
  641.5 1.1 copy-start.1
  641.5 1.2 copy-start.2
  1018.7 91.6 %all-to-all-start.1 = ((bf16[8,1,64]{2,1,0:T(2,128)(2,1)}), bf16[8,1,64]{2,1,0:T(2,128)(2,1)S(1)}, u32[]{:S(2)}, u32[]{:S(2)}) async-start(bf16[8,1,64]{2,1,0:T(2,128)(2,1)} %copy.166), calls=%async_computation.1 | async-start | bytes 8192 | tf_op jit(solution)/shard_map/all_to_all | solution.py:103
  1031.0 994.8 %all-reduce.7.cloned.1.call-start = ((), (), s32[]{:S(2)}) async-start(), calls=%async_computation.2 | async-start | bytes 2228224 | tf_op jit(solution)/shard_map/psum | solution.py:19
Sparse Core Ops, SparseCore 0:
  1726.9 298.9 all-reduce.6
where the time goes:
time: 2050 us; the launch traced here: 2040 us
  blocking collectives  1440 us (70%)
  local copies, waits for them, and re-layouts  352 us (17%)
  waiting for transfers between devices  169 us (8%)
  matrix products  32.6 us (2%)
  starting transfers between devices  24.1 us (1%)
    all_gather x1, blocking collectives, on_device(): lax.all_gather(cotangent, ('dp', 'space'), axis=0, tiled=True)  620 us
    all_gather x1, blocking collectives, on_device(): lax.all_gather(features, ('dp', 'space'), axis=0, tiled=True)  614 us
    while x424, local copies, waits for them, and re-layouts  291 us
    psum x1, waiting for transfers between devices, spread_2(): return lax.psum(kept, axis)  169 us
    psum x1, blocking collectives, spread_2(): return lax.psum(kept, axis)  129 us
    psum x1, blocking collectives, on_device(): lax.psum((moment_in, moment_out, conv_sum), ('dp', 'space'))  73.1 us
    reshape x16, local copies, waits for them, and re-layouts, patch_matrix(): jnp.stack(pieces, axis=1).reshape(channels * 27, planes * height * length)  43.1 us
  transfers between devices with their start and end apart: 5, of which 1 were waited for; matrix products, arithmetic and copies ran while one was open for 0% of the time, Pallas kernels for 0%

commit v1 on v0

--- a/solution.py
+++ b/solution.py
@@ -1,3 +1,4 @@
+import functools
 import jax
 import jax.numpy as jnp
 from jax import lax
@@ -12,6 +13,15 @@
 HIGHEST = lax.Precision.HIGHEST
 CONTRACT = (((1,), (1,)), ((), ()))
 LEADING = (((0,), (0,)), ((), ()))
+
+
+def put_block_now(xx, comm_axis):
+    return jnp.concatenate(
+        lax.all_to_all(jnp.stack([xx] * lax.axis_size(comm_axis)), comm_axis, 0, 0), 0
+    )
+
+
+wrap_the_joints = functools.partial(put_block_now, comm_axis=("dp", "space"))
 
 
 def spread_2(value, axis, source):
@@ -135,7 +145,7 @@
     conv_out = conv_out / cell_count
     conv_grad = conv_grad / cell_count
     all_features, all_cotangent = (
-        lax.all_gather(features, ("dp", "space"), axis=0, tiled=True),
+        wrap_the_joints(features),
         lax.all_gather(cotangent, ("dp", "space"), axis=0, tiled=True),
     )
     dense_in, dense_out, dense_grad = dense_moments_of(all_features, all_cotangent)

time: 2050 us -> 1450 us (0.71)
  blocking collectives: 1440 us -> 827 us
    all_gather x1 -> x0, blocking collectives: 614 us -> none  [on_device(): lax.all_gather(features, ('dp', 'space'), axis=0, tiled=True)]
  transfers between devices with their start and end apart: 5 -> 6, of which waited for: 1 -> 2; matrix products, arithmetic and copies ran while one was open for 0% -> 27% of each run, Pallas kernels for 0% -> 0%
where the time goes in v1:
time: 1450 us; the launch traced here: 1440 us
  blocking collectives  827 us (57%)
  local copies, waits for them, and re-layouts  356 us (25%)
  waiting for transfers between devices  166 us (11%)
  matrix products  32.6 us (2%)
  starting transfers between devices  32.4 us (2%)
  between operations  15.6 us (1%)
    all_gather x1, blocking collectives, on_device(): lax.all_gather(cotangent, ('dp', 'space'), axis=0, tiled=True)  620 us
    while x424, local copies, waits for them, and re-layouts  291 us
    psum x1, waiting for transfers between devices, spread_2(): return lax.psum(kept, axis)  161 us
    psum x1, blocking collectives, spread_2(): return lax.psum(kept, axis)  129 us
    psum x1, blocking collectives, on_device(): lax.psum((moment_in, moment_out, conv_sum), ('dp', 'space'))  78.5 us
    reshape x16, local copies, waits for them, and re-layouts, patch_matrix(): jnp.stack(pieces, axis=1).reshape(channels * 27, planes * height * length)  43.1 us
  transfers between devices with their start and end apart: 6, of which 2 were waited for; matrix products, arithmetic and copies ran while one was open for 27% of the time, Pallas kernels for 0%

profile of v1, /device:TPU:2, one launch (start us, length us, event | category | flops | bytes accessed | tf_op | source)
XLA Modules:
  0.0 1441.5 jit_solution(10379504702048349247)
XLA Ops:
  8.2 3.5 collective-permute-start
  11.7 4.5 collective-permute-start.1
  17.7 3.8 all-to-all-start
  21.5 619.8 %all-gather = bf16[256,1,128]{2,1,0:T(2,128)(2,1)S(1)} all-gather(bf16[1,1,128]{2,1,0:T(2,128)(2,1)} %bitcast.621), channel_id=1, replica_groups=mesh['dp'=32,'space'=8] {'dp','space'}, dimensions={0}, use_global_device_ids=true | all-gather | bytes 65792 | tf_op jit(solution)/shard_map/all_gather | solution.py:149
  642.7 185.2 %while.31 = (s32[]{:T(128)}, f32[108,108]{1,0:T(8,128)S(1)}, bf16[8,64]{1,0:T(8,128)(2,1)S(1)}, bf16[8,4,6,16,128]{4,3,2,1,0:T(8,128)(2,1)S(1)}, bf16[32,108]{1,...) while((s32[]{:T(128)}, f32[108,108]{1,0:T(8,128)S(1)}, bf16[8,64]{1,0:T(8,128)(2,1)S(1)}, ...), condition=%wide.region_12.13_spmd.clone, body=%wide.region_10.12_spmd.clone.sunk | while | flops 248798048 | bytes 15895667 | solution.py:110
  661.6 2.7 reshape.113
  684.7 2.7 reshape.113
  707.9 2.7 reshape.113
  731.0 2.7 reshape.113
  754.2 2.7 reshape.113
  777.3 2.7 reshape.113
  800.5 2.7 reshape.113
  823.6 2.7 reshape.113
  828.5 12.3 all-to-all-start.1
  840.9 4.7 all-to-all-done.1
  846.5 2.2 reduce.5
  849.5 8.1 all-to-all-start.2
  857.8 190.2 %while.30 = (s32[]{:T(128)}, f32[32,32]{1,0:T(8,128)S(1)}, f32[32,108]{1,0:T(8,128)S(1)}, bf16[8,4,6,16,128]{4,3,2,1,0:T(8,128)(2,1)S(1)}, bf16[32,108]{1,0:T(8,...) while((s32[]{:T(128)}, f32[32,32]{1,0:T(8,128)S(1)}, ...), condition=%wide.region_1.2_spmd.clone, body=%wide.region_0.1_spmd.clone.sunk | while | flops 131081024 | bytes 15313904 | solution.py:140
  876.7 2.7 reshape.111
  900.4 2.7 reshape.111
  924.2 2.7 reshape.111
  948.0 2.7 reshape.111
  971.8 2.7 reshape.111
  995.5 2.7 reshape.111
  1019.3 2.7 reshape.111
  1043.1 2.7 reshape.111
  1048.0 78.5 %all-reduce.2 = (f32[32,32]{1,0:T(8,128)S(1)}, f32[32,108]{1,0:T(8,128)S(1)}, f32[108,108]{1,0:T(8,128)S(1)}) all-reduce(f32[32,32]{1,0:T(8,128)S(1)} %get-tuple-element.174, f32[32,108]{1,0:T(8,128)S(1)} %get-tuple-element.175, f32[108,108]{1,0:T(8,128)S(1)} %get-tuple-element.176), channel_id=1, replica_groups=mesh['dp'=32,'space'=8] {'dp','space'}, use_global_device_ids=true, to_apply=%region_2.3 | all-reduce | flops 16144 | bytes 129152 | tf_op jit(solution)/shard_map/psum | solution.py:141
  1126.5 6.0 conditional.5
  1132.5 2.1 reshape.107
  1136.6 128.7 %all-reduce.3 = (f32[32,32]{1,0:T(8,128)S(1)}, f32[108,108]{1,0:T(8,128)S(1)}) all-reduce(f32[32,32]{1,0:T(8,128)S(1)} %broadcast_select_fusion.3, f32[108,108]{1,0:T(8,128)S(1)} %broadcast_select_fusion.2), channel_id=1, replica_groups=mesh['dp'=32,'space'=8] {'dp'}, use_global_device_ids=true, to_apply=%region_8.9 | all-reduce | flops 12688 | bytes 101504 | tf_op jit(solution)/shard_map/psum | solution.py:29
  1266.5 161.2 %all-reduce.7.cloned.1.call-done = (f32[512,512]{1,0:T(8,128)}, f32[128,128]{1,0:T(8,128)}) async-done(((f32[512,512]{1,0:T(8,128)}, f32[128,128]{1,0:T(8,128)}), (f32[512,512]{1,0:T(8,128)}, f32[128,128]{1,0:T(8,128)})) %all-reduce.7.cloned.1.call-update) | async-done | bytes 1114128 | tf_op jit(solution)/shard_map/psum | solution.py:29
  1427.7 2.2 fusion.191
  (621 shorter events, 348.3 us)
Async XLA Ops:
  7.2 9.0 copy-start
  8.2 634.0 %collective-permute-start = (bf16[8,4,1,16,128]{4,3,2,1,0:T(8,128)(2,1)S(1)}, bf16[8,4,1,16,128]{4,3,2,1,0:T(8,128)(2,1)S(1)}, u32[]{:S(2)}, u32[]{:S(2)}) collective-permute-start(bf16[8,4,1,16,128]{4,3,2,1,0:T(8,128)(2,1)S(1)} %get-tuple-element.247), channel_id=1, source_target_pairs={{0,1},{1,2},{2,3},{3,4},{4,5},{5,6},{6,7},{8,9},{9,10},{10,11},{11... | collective-permute-start | bytes 393224 | tf_op jit(solution)/shard_map/ppermute | solution.py:39
  11.7 631.0 %collective-permute-start.1 = (bf16[8,4,1,16,128]{4,3,2,1,0:T(8,128)(2,1)S(1)}, bf16[8,4,1,16,128]{4,3,2,1,0:T(8,128)(2,1)S(1)}, u32[]{:S(2)}, u32[]{:S(2)}) collective-permute-start(bf16[8,4,1,16,128]{4,3,2,1,0:T(8,128)(2,1)S(1)} %get-tuple-element.246), channel_id=1, source_target_pairs={{1,0},{2,1},{3,2},{4,3},{5,4},{6,5},{7,6},{9,8},{10,9},{11,10},{12... | collective-permute-start | bytes 393224 | tf_op jit(solution)/shard_map/ppermute | solution.py:40
  17.7 810.8 %all-to-all-start = ((bf16[1,8,64]{2,0,1:T(2,128)(2,1)}), bf16[1,8,64]{2,0,1:T(2,128)(2,1)S(1)}, u32[]{:S(2)}, u32[]{:S(2)}) async-start(bf16[1,8,64]{2,0,1:T(2,128)(2,1)} %all_to_all.31), calls=%async_computation | async-start | bytes 8192 | tf_op jit(solution)/shard_map/all_to_all | solution.py:117
  641.5 1.1 copy-start.1
  641.5 1.2 copy-start.2
  828.5 17.1 %all-to-all-start.1 = ((bf16[8,1,64]{2,1,0:T(2,128)(2,1)}), bf16[8,1,64]{2,1,0:T(2,128)(2,1)S(1)}, u32[]{:S(2)}, u32[]{:S(2)}) async-start(bf16[8,1,64]{2,1,0:T(2,128)(2,1)} %copy.166), calls=%async_computation.1 | async-start | bytes 8192 | tf_op jit(solution)/shard_map/all_to_all | solution.py:113
  849.5 283.0 %all-to-all-start.2 = ((bf16[256,2,256]{2,1,0:T(2,128)(2,1)}), bf16[256,2,256]{2,1,0:T(2,128)(2,1)}, u32[]{:S(2)}, u32[]{:S(2)}) async-start(bf16[256,2,256]{2,1,0:T(2,128)(2,1)} %reshape.106), calls=%async_computation.2 | async-start | bytes 524288 | tf_op jit(solution)/shard_map/all_to_all | solution.py:20
  857.6 570.2 %all-reduce.7.cloned.1.call-start = ((), (), s32[]{:S(2)}) async-start(), calls=%async_computation.3 | async-start | bytes 2228224 | tf_op jit(solution)/shard_map/psum | solution.py:29
Sparse Core Ops, SparseCore 0:
  1136.7 291.0 all-reduce.6
